TPU v7x, 32 devices: a whole 2x2x4 slice. The times are simulated.
32 devices in a mesh: wide: 16 (over z, y, core), narrow: 2 (over x).
Axes of the slice: x: 2, y: 2, z: 4, core: 2. Of those that a mesh axis runs over, the one named last changes fastest.
Arguments:
- concentrations: float32 [256, 32, 256], P('wide', 'narrow'), may hold values from 0.1 to 2
- wind_speeds: bfloat16 [2, 2, 32, 256], P(None, None, ('narrow', 'wide')), may hold values from -0.59765625 to 0.59765625
- rate_constants: float32 [768], replicated, may hold values from 0.05 to 1
- reactants: int32 [768, 2], replicated, may hold values from 0 to 255
- products: int32 [768, 2], replicated, may hold values from 0 to 255
Outputs:
- after_chemistry: float32 [256, 32, 256], P(None, ('narrow', 'wide'))
Inputs may be any that keep to these rules, and one draw needn't show every extreme that they name: `reactants`: each entry is a species number. `products`: each entry is a species number.
All inputs are finite; a program needn't handle non-finite values.
Results may differ from a plain program's by a relative error of at most 0.0003.
Values may be sent and summed in bfloat16 or wider, within the bound.
A program may use at most 64 MiB of HBM per device.

v0:
```python
import jax
import jax.numpy as jnp
from jax import lax
from jax.sharding import PartitionSpec as P

S = 256
SUB = 2
SECTIONS = 6
DIFFUSION = 0.1
CHEM_STEP = 0.02


def padded(cells, sides, width):
    for axis, dim in sides:
        count = lax.axis_size(axis)
        head = lax.slice_in_dim(cells, 0, width, axis=dim)
        tail = lax.slice_in_dim(cells, cells.shape[dim] - width, cells.shape[dim], axis=dim)
        cells = jnp.concatenate(
            [
                lax.ppermute(tail, axis, [(i, (i + 1) % count) for i in range(count)]),
                cells,
                lax.ppermute(head, axis, [((i + 1) % count, i) for i in range(count)]),
            ],
            axis=dim,
        )
    return cells


def take_range(array, begin_at, end_at, along):
    along = along % array.ndim
    index = [slice(None)] * array.ndim
    index[along] = slice(begin_at, end_at)
    return array[tuple(index)]


def minmod(first_jump, second_jump):
    return jnp.maximum(0.0, jnp.minimum(first_jump, second_jump)) + jnp.minimum(
        0.0, jnp.maximum(first_jump, second_jump)
    )


def sweep_axis(extended, speeds, along, closed):
    length = extended.shape[along]
    speed_face = 0.5 * (
        take_range(speeds, 0, length - 1, along) + take_range(speeds, 1, length, along)
    )
    jumps = take_range(extended, 1, length, along) - take_range(extended, 0, length - 1, along)
    slopes = minmod(
        take_range(jumps, 0, length - 2, along), take_range(jumps, 1, length - 1, along)
    )
    inner_speed = take_range(speed_face, 1, length - 2, along)
    left_value = take_range(extended, 1, length - 2, along) + 0.5 * (
        1.0 - inner_speed
    ) * take_range(slopes, 0, length - 3, along)
    right_value = take_range(extended, 2, length - 1, along) - 0.5 * (
        1.0 + inner_speed
    ) * take_range(slopes, 1, length - 2, along)
    face_flux = inner_speed * jnp.where(
        inner_speed >= 0.0, left_value, right_value
    ) - DIFFUSION * take_range(jumps, 1, length - 2, along)
    if closed:
        position = lax.broadcasted_iota(jnp.int32, face_flux.shape, along % face_flux.ndim)
        face_flux = jnp.where((position > 0) & (position < length - 4), face_flux, 0.0)
    return take_range(extended, 2, length - 2, along) - (
        take_range(face_flux, 1, length - 3, along) - take_range(face_flux, 0, length - 4, along)
    )


def sweep_second(tracer, speeds):
    pad_tracer = [(0, 0)] * (tracer.ndim - 1) + [(2, 2)]
    pad_speeds = [(0, 0)] * (speeds.ndim - 1) + [(2, 2)]
    return sweep_axis(
        jnp.pad(tracer, pad_tracer, mode="edge"), jnp.pad(speeds, pad_speeds, mode="edge"), -1, True
    )


def react_cells(cell_block, rate_constants, first_ids, second_ids, net_matrix):
    for section_index in range(SECTIONS):
        rate_values = (
            rate_constants[:, None]
            * jnp.take(cell_block, first_ids, axis=0)
            * jnp.take(cell_block, second_ids, axis=0)
        )
        cell_block = cell_block + CHEM_STEP * jnp.dot(
            net_matrix, rate_values, precision=lax.Precision.HIGHEST
        )
    return cell_block


def on_device(concentrations, wind_speeds, rate_constants, reactants, products):
    groups = concentrations.shape[0]
    row_count = wind_speeds.shape[2]
    columns = wind_speeds.shape[3]
    wide_count = lax.axis_size("wide")
    planes = wind_speeds.reshape(SUB * 2, row_count, columns)
    gathered = lax.all_gather(planes, "wide", axis=1, tiled=True).astype(jnp.float32)
    tracer = concentrations
    stacked = jnp.concatenate([tracer, gathered], 0)
    extended = padded(stacked, (("narrow", 1),), 4)
    wind_rims = extended[groups:]
    tracer = sweep_axis(extended[:groups], wind_rims[0], -2, False)
    tracer = sweep_second(tracer, wind_rims[1, 2:-2])
    tracer = sweep_axis(tracer, wind_rims[2, 2:-2], -2, False)
    tracer = sweep_second(tracer, wind_rims[3, 4:-4])
    species_ids = lax.broadcasted_iota(jnp.int32, (S, rate_constants.shape[0]), 0)

    def one_hot(species_column):
        return (species_ids == species_column[None, :]).astype(jnp.float32)

    net_matrix = (
        one_hot(products[:, 0])
        + one_hot(products[:, 1])
        - one_hot(reactants[:, 0])
        - one_hot(reactants[:, 1])
    )
    first_ids = reactants[:, 0]
    second_ids = reactants[:, 1]
    shaped = tracer.reshape(groups, wide_count, row_count, columns)
    cell_block = lax.all_to_all(shaped, "wide", split_axis=1, concat_axis=0, tiled=True)
    flattened = cell_block.reshape(cell_block.shape[0], -1)
    regrouped = react_cells(flattened, rate_constants, first_ids, second_ids, net_matrix).reshape(
        cell_block.shape
    )
    return regrouped.reshape(S, row_count, columns)


def solution(mesh):
    return jax.shard_map(
        on_device,
        mesh=mesh,
        in_specs=(
            P("wide", "narrow", None),
            P(None, None, ("narrow", "wide"), None),
            P(),
            P(),
            P(),
        ),
        out_specs=P(None, ("narrow", "wide"), None),
        check_vma=False,
    )
```

profile of v0, /device:TPU:0, one launch (start us, length us, event | category | flops | bytes accessed | tf_op | source)
XLA Modules:
  0.0 136.4 jit_solution(5072353564964290958)
XLA Ops:
  0.7 23.2 %all_gather.3 = bf16[4,16,256]{2,0,1:T(4,128)(2,1)S(1)} all-gather(bf16[4,1,256]{2,0,1:T(4,128)(2,1)S(1)} %reshape.84), channel_id=1, replica_groups=mesh['wide'=16,'narrow'=2] {'wide'}, dimensions={1}, use_global_device_ids=true | all-gather | bytes 34816 | tf_op jit(solution)/shard_map/all_gather | solution.py:96
  38.3 2.5 %copy.88 = f32[16,23,256]{1,0,2:T(8,128)} copy(f32[16,23,256]{2,1,0:T(8,128)S(1)} %get-tuple-element.29) | data formatting | bytes 753664
  40.8 2.5 %copy.89 = f32[16,23,256]{1,0,2:T(8,128)} copy(f32[16,23,256]{2,1,0:T(8,128)S(1)} %get-tuple-element.28) | data formatting | bytes 753664
  43.2 2.5 %sub.79 = f32[16,23,256]{1,0,2:T(8,128)S(1)} subtract(f32[16,23,256]{1,0,2:T(8,128)} %copy.88, f32[16,23,256]{1,0,2:T(8,128)} %copy.89) | non-fusion elementwise | flops 94208 | bytes 1130496 | tf_op jit(solution)/shard_map/sub | solution.py:47
  47.6 2.5 %copy.87 = f32[16,21,256]{1,0,2:T(8,128)} copy(f32[16,21,256]{2,1,0:T(8,128)S(1)} %get-tuple-element.26) | data formatting | bytes 688128
  50.1 2.5 %copy.90 = f32[16,21,256]{1,0,2:T(8,128)} copy(f32[16,21,256]{2,1,0:T(8,128)S(1)} %get-tuple-element.27) | data formatting | bytes 688128
  54.4 2.5 %copy.86 = f32[16,20,256]{1,0,2:T(8,128)} copy(f32[16,20,256]{2,1,0:T(8,128)S(1)} %slice.393) | data formatting | bytes 655360
  56.9 4.8 %fusion.22 = f32[16,21,256]{1,0,2:T(8,128)S(1)} fusion(f32[16,23,256]{1,0,2:T(8,128)S(1)} %sub.79, f32[16,21,256]{1,0,2:T(8,128)} %copy.90, f32[16,22,256]{1,0,2:T(8,128)} %minimum_add_fusion.3, f32[16,21,256]{1,0,2:T(8,128)} %copy.87, f32[21,256]{0,1:T(8,128)S(1)} %copy.70, f32[21,256]{0,1:T(8,128)S(1)} %copy.66, f32[21,256]{0,1:T(8,128)S(1)} %copy-done.7, ...), kind=kLoop, calls=%fused_computation.59 | loop fusion | flops 688128 | bytes 2134272 | tf_op jit(solution)/shard_map/sub | solution.py:58
  65.9 6.3 %fusion.7 = f32[16,20,257]{1,0,2:T(8,128)S(1)} fusion(f32[16,20,259]{1,0,2:T(8,128)S(1)} %slice_subtract_fusion.1, f32[16,20,258]{1,0,2:T(8,128)} %minimum_add_fusion.1, f32[16,20,2]{1,0,2:T(8,128)S(1)} %reshape.88, f32[16,20,256]{1,0,2:T(8,128)} %copy-done, f32[16,20,2]{1,0,2:T(8,128)S(1)} %reshape.87, f32[20,257]{0,1:T(8,128)S(1)} %copy.74, ...), kind=kLoop, calls=%fused_computation.31 | loop fusion | flops 904640 | bytes 1715717 | tf_op jit(solution)/shard_map/jit(_where)/select_n | solution.py:63
  75.5 5.1 %fusion.15 = f32[16,17,256]{1,0,2:T(8,128)S(1)} fusion(f32[16,19,256]{1,0,2:T(8,128)} %copy-done.2, f32[16,18,256]{1,0,2:T(8,128)} %minimum_add_fusion.2, f32[16,20,256]{1,0,2:T(8,128)S(1)} %fusion.20, f32[17,256]{0,1:T(8,128)S(1)} %copy.78, f32[17,256]{0,1:T(8,128)S(1)} %copy.77, f32[17,256]{0,1:T(8,128)S(1)} %copy-done.6, pred[17,256]{0,1:T(8,128)(4,1)S(1)} %copy.76), kind=kLoop, calls=%fused_computation.46 | loop fusion | flops 557056 | bytes 1727744 | tf_op jit(solution)/shard_map/sub | solution.py:58
  83.0 2.8 %fusion.1 = f32[16,16,257]{1,0,2:T(8,128)S(1)} fusion(f32[16,16,259]{1,0,2:T(8,128)S(1)} %slice_subtract_fusion, f32[16,16,258]{1,0,2:T(8,128)S(1)} %minimum_add_fusion, f32[16,16,2]{1,0,2:T(8,128)S(1)} %reshape.92, f32[16,16,256]{1,0,2:T(8,128)S(1)} %fusion.14, f32[16,16,2]{1,0,2:T(8,128)S(1)} %reshape.91, f32[16,257]{0,1:T(8,128)S(1)} %copy-done.4, ...), kind=kLoop, calls=%fused_computation.20 | loop fusion | flops 723712 | bytes 1372625 | tf_op jit(solution)/shard_map/jit(_where)/select_n | solution.py:63
  88.0 3.8 %all-to-all-start = ((f32[16,16,1,256]{3,0,2,1:T(8,128)}), f32[16,16,1,256]{3,0,2,1:T(8,128)S(1)}, u32[]{:S(2)}, u32[]{:S(2)}) async-start(f32[16,16,1,256]{3,0,2,1:T(8,128)} %copy.83), calls=%async_computation | async-start | bytes 524288 | tf_op jit(solution)/shard_map/all_to_all | solution.py:119
  91.9 9.7 %all-to-all-done = f32[16,16,1,256]{3,0,2,1:T(8,128)S(1)} async-done(((f32[16,16,1,256]{3,0,2,1:T(8,128)}), f32[16,16,1,256]{3,0,2,1:T(8,128)S(1)}, u32[]{:S(2)}, u32[]{:S(2)}) %all-to-all-start) | async-done | bytes 262176 | tf_op jit(solution)/shard_map/all_to_all | solution.py:119
  103.6 2.1 %gather_fusion.1 = f32[768,256]{1,0:T(8,128)S(1)} fusion(f32[256,256]{1,0:T(8,128)S(1)} %bitcast.31, s32[1024]{0:T(1024)S(1)} %pad_clamp_fusion), kind=kCustom, calls=%fused_computation.1.clone | custom fusion | bytes 1575936 | tf_op jit(solution)/shard_map/jit(_take)/gather | solution.py:82
  107.1 2.1 %gather_fusion.2 = f32[768,256]{1,0:T(8,128)S(1)} fusion(f32[256,256]{1,0:T(8,128)S(1)} %fusion.32, s32[1024]{0:T(1024)S(1)} %pad_clamp_fusion.1), kind=kCustom, calls=%fused_computation.2.clone | custom fusion | bytes 1575936 | tf_op jit(solution)/shard_map/jit(_take)/gather | solution.py:81
  109.3 2.1 %gather_fusion.3 = f32[768,256]{1,0:T(8,128)S(1)} fusion(f32[256,256]{1,0:T(8,128)S(1)} %fusion.32, s32[1024]{0:T(1024)S(1)} %pad_clamp_fusion), kind=kCustom, calls=%fused_computation.3.clone | custom fusion | bytes 1575936 | tf_op jit(solution)/shard_map/jit(_take)/gather | solution.py:82
  112.7 2.1 %gather_fusion.4 = f32[768,256]{1,0:T(8,128)S(1)} fusion(f32[256,256]{1,0:T(8,128)S(1)} %fusion.31, s32[1024]{0:T(1024)S(1)} %pad_clamp_fusion.1), kind=kCustom, calls=%fused_computation.4.clone | custom fusion | bytes 1575936 | tf_op jit(solution)/shard_map/jit(_take)/gather | solution.py:81
  114.9 2.1 %gather_fusion.5 = f32[768,256]{1,0:T(8,128)S(1)} fusion(f32[256,256]{1,0:T(8,128)S(1)} %fusion.31, s32[1024]{0:T(1024)S(1)} %pad_clamp_fusion), kind=kCustom, calls=%fused_computation.5.clone | custom fusion | bytes 1575936 | tf_op jit(solution)/shard_map/jit(_take)/gather | solution.py:82
  118.4 2.1 %gather_fusion.6 = f32[768,256]{1,0:T(8,128)S(1)} fusion(f32[256,256]{1,0:T(8,128)S(1)} %fusion.30, s32[1024]{0:T(1024)S(1)} %pad_clamp_fusion.1), kind=kCustom, calls=%fused_computation.6.clone | custom fusion | bytes 1575936 | tf_op jit(solution)/shard_map/jit(_take)/gather | solution.py:81
  120.5 2.1 %gather_fusion.7 = f32[768,256]{1,0:T(8,128)S(1)} fusion(f32[256,256]{1,0:T(8,128)S(1)} %fusion.30, s32[1024]{0:T(1024)S(1)} %pad_clamp_fusion), kind=kCustom, calls=%fused_computation.7.clone | custom fusion | bytes 1575936 | tf_op jit(solution)/shard_map/jit(_take)/gather | solution.py:82
  124.0 2.1 %gather_fusion.8 = f32[768,256]{1,0:T(8,128)S(1)} fusion(f32[256,256]{1,0:T(8,128)S(1)} %fusion.29, s32[1024]{0:T(1024)S(1)} %pad_clamp_fusion.1), kind=kCustom, calls=%fused_computation.8.clone | custom fusion | bytes 1575936 | tf_op jit(solution)/shard_map/jit(_take)/gather | solution.py:81
  126.1 2.4 %gather_fusion.9 = f32[768,256]{1,0:T(8,128)S(1)} fusion(f32[256,256]{1,0:T(8,128)S(1)} %fusion.29, s32[1024]{0:T(1024)S(1)} %pad_clamp_fusion), kind=kCustom, calls=%fused_computation.9.clone | custom fusion | bytes 1575936 | tf_op jit(solution)/shard_map/jit(_take)/gather | solution.py:82
  129.8 2.1 %gather_fusion.10 = f32[768,256]{1,0:T(8,128)S(1)} fusion(f32[256,256]{1,0:T(8,128)S(1)} %fusion.28, s32[1024]{0:T(1024)S(1)} %pad_clamp_fusion.1), kind=kCustom, calls=%fused_computation.10.clone | custom fusion | bytes 1575936 | tf_op jit(solution)/shard_map/jit(_take)/gather | solution.py:81
  131.9 2.1 %gather_fusion.11 = f32[768,256]{1,0:T(8,128)S(1)} fusion(f32[256,256]{1,0:T(8,128)S(1)} %fusion.28, s32[1024]{0:T(1024)S(1)} %pad_clamp_fusion), kind=kCustom, calls=%fused_computation.11.clone | custom fusion | bytes 1575936 | tf_op jit(solution)/shard_map/jit(_take)/gather | solution.py:82
  (127 shorter events, 41.8 us)
Async XLA Ops:
  24.9 6.4 %collective-permute-start = (f32[20,4,256]{2,1,0:T(4,128)S(1)}, f32[20,4,256]{2,1,0:T(4,128)S(1)}, u32[]{:S(2)}, u32[]{:S(2)}) collective-permute-start(f32[20,4,256]{2,1,0:T(4,128)S(1)} %get-tuple-element.30), channel_id=1, source_target_pairs={{0,1},{1,0},{2,3},{3,2},{4,5},{5,4},{6,7},{7,6},{8,9},{9,8},{10,11... | collective-permute-start | bytes 245768 | tf_op jit(solution)/shard_map/ppermute | solution.py:20
  26.5 5.0 %collective-permute-start.1 = (f32[20,4,256]{2,1,0:T(4,128)S(1)}, f32[20,4,256]{2,1,0:T(4,128)S(1)}, u32[]{:S(2)}, u32[]{:S(2)}) collective-permute-start(f32[20,4,256]{2,1,0:T(4,128)S(1)} %get-tuple-element.31), channel_id=1, source_target_pairs={{1,0},{0,1},{3,2},{2,3},{5,4},{4,5},{7,6},{6,7},{9,8},{8,9},{11,10... | collective-permute-start | bytes 245768 | tf_op jit(solution)/shard_map/ppermute | solution.py:22
  50.1 2.5 %copy-start.13 = (f32[21,256]{1,0:T(8,128)S(1)}, f32[21,256]{1,0:T(8,128)}, u32[]{:S(2)}) copy-start(f32[21,256]{1,0:T(8,128)} %get-tuple-element.42) | copy-start | bytes 64516
  50.1 6.8 %copy-start.7 = (f32[21,256]{0,1:T(8,128)S(1)}, f32[21,256]{0,1:T(8,128)}, u32[]{:S(2)}) copy-start(f32[21,256]{0,1:T(8,128)} %copy.63) | copy-start | bytes 64516
  56.9 4.8 %copy-start.3 = (f32[16,20,256]{1,0,2:T(8,128)S(1)}, f32[16,20,256]{1,0,2:T(8,128)}, u32[]{:S(2)}) copy-start(f32[16,20,256]{1,0,2:T(8,128)} %copy.86) | copy-start | bytes 983044
  62.3 1.3 copy-start
  63.8 1.7 %copy-start.9 = (f32[20,257]{1,0:T(8,128)S(1)}, f32[20,257]{1,0:T(8,128)}, u32[]{:S(2)}) copy-start(f32[20,257]{1,0:T(8,128)} %get-tuple-element.32) | copy-start | bytes 61684
  63.8 1.8 %copy-start.8 = (f32[20,257]{1,0:T(8,128)S(1)}, f32[20,257]{1,0:T(8,128)}, u32[]{:S(2)}) copy-start(f32[20,257]{1,0:T(8,128)} %get-tuple-element.33) | copy-start | bytes 61684
  63.8 1.9 %copy-start.14 = (pred[20,257]{1,0:T(8,128)(4,1)S(1)}, pred[20,257]{1,0:T(8,128)(4,1)}, u32[]{:S(2)}) copy-start(pred[20,257]{1,0:T(8,128)(4,1)} %get-tuple-element.18) | copy-start | bytes 15424
  63.8 2.1 %copy-start.5 = (f32[20,257]{0,1:T(8,128)S(1)}, f32[20,257]{0,1:T(8,128)}, u32[]{:S(2)}) copy-start(f32[20,257]{0,1:T(8,128)} %copy.71) | copy-start | bytes 61684
  63.8 2.1 %copy-start.19 = (pred[257]{0:T(512)(128)(4,1)S(1)}, pred[257]{0:T(512)(128)(4,1)}, u32[]{:S(2)}) copy-start(pred[257]{0:T(512)(128)(4,1)} %fusion.90) | copy-start | bytes 775
  65.9 6.4 %copy-start.1 = (f32[16,20,256]{1,0,2:T(8,128)S(1)}, f32[16,20,256]{1,0,2:T(8,128)}, u32[]{:S(2)}) copy-start(f32[16,20,256]{1,0,2:T(8,128)} %copy-done) | copy-start | bytes 983044
  73.1 2.0 %copy-start.2 = (f32[16,19,256]{1,0,2:T(8,128)}, f32[16,19,256]{1,0,2:T(8,128)S(1)}, u32[]{:S(2)}) copy-start(f32[16,19,256]{1,0,2:T(8,128)S(1)} %slice_subtract_fusion.4) | copy-start | bytes 933892
  73.2 2.0 %copy-start.12 = (f32[17,256]{1,0:T(8,128)S(1)}, f32[17,256]{1,0:T(8,128)}, u32[]{:S(2)}) copy-start(f32[17,256]{1,0:T(8,128)} %get-tuple-element.40) | copy-start | bytes 52228
  73.2 2.1 %copy-start.11 = (f32[17,256]{1,0:T(8,128)S(1)}, f32[17,256]{1,0:T(8,128)}, u32[]{:S(2)}) copy-start(f32[17,256]{1,0:T(8,128)} %get-tuple-element.41) | copy-start | bytes 52228
  73.2 2.2 %copy-start.15 = (pred[17,256]{1,0:T(8,128)(4,1)S(1)}, pred[17,256]{1,0:T(8,128)(4,1)}, u32[]{:S(2)}) copy-start(pred[17,256]{1,0:T(8,128)(4,1)} %get-tuple-element.16) | copy-start | bytes 13060
  73.2 2.3 %copy-start.6 = (f32[17,256]{0,1:T(8,128)S(1)}, f32[17,256]{0,1:T(8,128)}, u32[]{:S(2)}) copy-start(f32[17,256]{0,1:T(8,128)} %copy.75) | copy-start | bytes 52228
  82.1 0.9 copy-start.4
  82.1 0.9 copy-start.10
  86.2 5.6 %copy-start.17 = (s32[768]{0:T(1024)S(1)}, s32[768]{0:T(1024)}, u32[]{:S(2)}) copy-start(s32[768]{0:T(1024)} %get-tuple-element.45) | copy-start | bytes 9220
  86.2 5.6 %copy-start.16 = (s32[768]{0:T(1024)S(1)}, s32[768]{0:T(1024)}, u32[]{:S(2)}) copy-start(s32[768]{0:T(1024)} %get-tuple-element.44) | copy-start | bytes 9220
  86.2 5.6 %copy-start.18 = (s32[768,2]{0,1:T(2,128)S(1)}, s32[768,2]{0,1:T(2,128)}, u32[]{:S(2)}) copy-start(s32[768,2]{0,1:T(2,128)} %param.11) | copy-start | bytes 18436
  88.0 13.5 %all-to-all-start = ((f32[16,16,1,256]{3,0,2,1:T(8,128)}), f32[16,16,1,256]{3,0,2,1:T(8,128)S(1)}, u32[]{:S(2)}, u32[]{:S(2)}) async-start(f32[16,16,1,256]{3,0,2,1:T(8,128)} %copy.83), calls=%async_computation | async-start | bytes 524288 | tf_op jit(solution)/shard_map/all_to_all | solution.py:119
  103.6 2.1 %copy-start.20 = (f32[768]{0:T(1024)S(1)}, f32[768]{0:T(1024)}, u32[]{:S(2)}) copy-start(f32[768]{0:T(1024)} %param.9) | copy-start | bytes 9220
where the time goes:
time: 137 us; the launch traced here: 136 us
  local copies, waits for them, and re-layouts  52.4 us (38%)
  other arithmetic  36.3 us (26%)
  blocking collectives  23.2 us (17%)
  waiting for transfers between devices  9.79 us (7%)
  matrix products  8.2 us (6%)
  starting transfers between devices  5.84 us (4%)
    all_gather x1, blocking collectives, on_device(): lax.all_gather(planes, 'wide', axis=1, tiled=True).astype(jnp.float32)  23.2 us
    unnamed x49, local copies, waits for them, and re-layouts  15.1 us
    gather x6, local copies, waits for them, and re-layouts, react_cells(): jnp.take(cell_block, second_ids, axis=0)  12.9 us
    gather x6, local copies, waits for them, and re-layouts, react_cells(): jnp.take(cell_block, first_ids, axis=0)  12.6 us
    sub x2, other arithmetic, sweep_axis(): inner_speed * jnp.where(inner_speed >= 0.0, left_value, right_value)  9.84 us
    all_to_all x1, waiting for transfers between devices, on_device(): lax.all_to_all(shaped, 'wide', split_axis=1, concat_axis=0, tiled=True)  9.66 us
    select_n x2, other arithmetic, sweep_axis(): jnp.where((position > 0) & (position < length - 4), face_flux, 0.0)  9.12 us
    dot_general x6, matrix products, react_cells(): jnp.dot(net_matrix, rate_values, precision=lax.Precision.HIGHEST)  8.2 us
  transfers between devices with their start and end apart: 3, of which 2 were waited for; matrix products, arithmetic and copies ran while one was open for 3% of the time, Pallas kernels for 0%

commit v1 on v0

--- a/solution.py
+++ b/solution.py
@@ -93,7 +93,9 @@
     columns = wind_speeds.shape[3]
     wide_count = lax.axis_size("wide")
     planes = wind_speeds.reshape(SUB * 2, row_count, columns)
-    gathered = lax.all_gather(planes, "wide", axis=1, tiled=True).astype(jnp.float32)
+    gathered = jnp.concatenate(
+        lax.all_to_all(jnp.stack([planes] * lax.axis_size("wide")), "wide", 0, 0), axis=1
+    ).astype(jnp.float32)
     tracer = concentrations
     stacked = jnp.concatenate([tracer, gathered], 0)
     extended = padded(stacked, (("narrow", 1),), 4)

time: 137 us -> 127 us (0.927)
  blocking collectives: 23.2 us -> 0 us
  starting transfers between devices: 5.84 us -> 13.3 us
  waiting for transfers between devices: 9.79 us -> 15.1 us
    all_gather x1 -> x0, blocking collectives: 23.2 us -> none  [on_device(): lax.all_gather(planes, 'wide', axis=1, tiled=True).astype(jnp.float32)]
    all_to_all x0 -> x1, starting transfers between devices: none -> 7.41 us  [on_device(): lax.all_to_all(jnp.stack([planes] * lax.axis_size('wide')), 'wide', 0, 0)]
    all_to_all x0 -> x1, waiting for transfers between devices: none -> 3.7 us  [on_device(): lax.all_to_all(jnp.stack([planes] * lax.axis_size('wide')), 'wide', 0, 0)]
  transfers between devices with their start and end apart: 3 -> 4, of which waited for: 2 -> 4; matrix products, arithmetic and copies ran while one was open for 3% -> 4% of each run, Pallas kernels for 0% -> 0%
where the time goes in v1:
time: 127 us
  local copies, waits for them, and re-layouts  53.1 us (42%)
  other arithmetic  36.2 us (29%)
  waiting for transfers between devices  15.1 us (12%)
  starting transfers between devices  13.3 us (10%)
  matrix products  8.2 us (6%)
    unnamed x49, local copies, waits for them, and re-layouts  15.2 us
    gather x6, local copies, waits for them, and re-layouts, react_cells(): jnp.take(cell_block, second_ids, axis=0)  12.9 us
    gather x6, local copies, waits for them, and re-layouts, react_cells(): jnp.take(cell_block, first_ids, axis=0)  12.6 us
    sub x2, other arithmetic, sweep_axis(): inner_speed * jnp.where(inner_speed >= 0.0, left_value, right_value)  9.84 us
    all_to_all x1, waiting for transfers between devices, on_device(): lax.all_to_all(shaped, 'wide', split_axis=1, concat_axis=0, tiled=True)  9.66 us
    select_n x2, other arithmetic, sweep_axis(): jnp.where((position > 0) & (position < length - 4), face_flux, 0.0)  9.11 us
    dot_general x6, matrix products, react_cells(): jnp.dot(net_matrix, rate_values, precision=lax.Precision.HIGHEST)  8.2 us
    all_to_all x1, starting transfers between devices, on_device(): lax.all_to_all(jnp.stack([planes] * lax.axis_size('wide')), 'wide', 0, 0)  7.41 us
  transfers between devices with their start and end apart: 4, of which 4 were waited for; matrix products, arithmetic and copies ran while one was open for 4% of the time, Pallas kernels for 0%

profile of v1, /device:TPU:0, one launch (start us, length us, event | category | flops | bytes accessed | tf_op | source)
XLA Modules:
  0.0 126.7 jit_solution(13693207859035510798)
XLA Ops:
  1.3 7.4 %all-to-all-start = ((bf16[16,4,1,256]{3,1,2,0:T(4,128)(2,1)}), bf16[16,4,1,256]{3,1,2,0:T(4,128)(2,1)S(1)}, u32[]{:S(2)}, u32[]{:S(2)}) async-start(bf16[16,4,1,256]{3,1,2,0:T(4,128)(2,1)} %stack.3), calls=%async_computation | async-start | bytes 65536 | tf_op jit(solution)/shard_map/all_to_all | solution.py:97
  11.7 3.7 %all-to-all-done = bf16[16,4,1,256]{3,1,2,0:T(4,128)(2,1)S(1)} async-done(((bf16[16,4,1,256]{3,1,2,0:T(4,128)(2,1)}), bf16[16,4,1,256]{3,1,2,0:T(4,128)(2,1)S(1)}, u32[]{:S(2)}, u32[]{:S(2)}) %all-to-all-start) | async-done | bytes 32800 | tf_op jit(solution)/shard_map/all_to_all | solution.py:97
  28.5 2.5 %copy.79 = f32[16,23,256]{1,0,2:T(8,128)} copy(f32[16,23,256]{2,1,0:T(8,128)S(1)} %get-tuple-element.29) | data formatting | bytes 753664
  31.0 2.5 %copy.80 = f32[16,23,256]{1,0,2:T(8,128)} copy(f32[16,23,256]{2,1,0:T(8,128)S(1)} %get-tuple-element.28) | data formatting | bytes 753664
  33.4 2.5 %sub.79 = f32[16,23,256]{1,0,2:T(8,128)S(1)} subtract(f32[16,23,256]{1,0,2:T(8,128)} %copy.79, f32[16,23,256]{1,0,2:T(8,128)} %copy.80) | non-fusion elementwise | flops 94208 | bytes 1130496 | tf_op jit(solution)/shard_map/sub | solution.py:47
  37.8 2.5 %copy.78 = f32[16,21,256]{1,0,2:T(8,128)} copy(f32[16,21,256]{2,1,0:T(8,128)S(1)} %get-tuple-element.26) | data formatting | bytes 688128
  40.4 2.5 %copy.81 = f32[16,21,256]{1,0,2:T(8,128)} copy(f32[16,21,256]{2,1,0:T(8,128)S(1)} %get-tuple-element.27) | data formatting | bytes 688128
  44.6 2.5 %copy.77 = f32[16,20,256]{1,0,2:T(8,128)} copy(f32[16,20,256]{2,1,0:T(8,128)S(1)} %slice.394) | data formatting | bytes 655360
  47.2 4.8 %fusion.22 = f32[16,21,256]{1,0,2:T(8,128)S(1)} fusion(f32[16,23,256]{1,0,2:T(8,128)S(1)} %sub.79, f32[16,21,256]{1,0,2:T(8,128)} %copy.81, f32[16,22,256]{1,0,2:T(8,128)} %minimum_add_fusion.3, f32[16,21,256]{1,0,2:T(8,128)} %copy.78, f32[21,256]{0,1:T(8,128)S(1)} %copy.61, f32[21,256]{0,1:T(8,128)S(1)} %copy.57, f32[21,256]{0,1:T(8,128)S(1)} %copy-done.7, ...), kind=kLoop, calls=%fused_computation.59 | loop fusion | flops 688128 | bytes 2134272 | tf_op jit(solution)/shard_map/sub | solution.py:58
  56.1 6.3 %fusion.7 = f32[16,20,257]{1,0,2:T(8,128)S(1)} fusion(f32[16,20,259]{1,0,2:T(8,128)S(1)} %slice_subtract_fusion.1, f32[16,20,258]{1,0,2:T(8,128)} %minimum_add_fusion.1, f32[16,20,2]{1,0,2:T(8,128)S(1)} %reshape.93, f32[16,20,256]{1,0,2:T(8,128)} %copy-done, f32[16,20,2]{1,0,2:T(8,128)S(1)} %reshape.92, f32[20,257]{0,1:T(8,128)S(1)} %copy.65, ...), kind=kLoop, calls=%fused_computation.31 | loop fusion | flops 904640 | bytes 1715717 | tf_op jit(solution)/shard_map/jit(_where)/select_n | solution.py:63
  65.7 5.1 %fusion.15 = f32[16,17,256]{1,0,2:T(8,128)S(1)} fusion(f32[16,19,256]{1,0,2:T(8,128)} %copy-done.2, f32[16,18,256]{1,0,2:T(8,128)} %minimum_add_fusion.2, f32[16,20,256]{1,0,2:T(8,128)S(1)} %fusion.20, f32[17,256]{0,1:T(8,128)S(1)} %copy.69, f32[17,256]{0,1:T(8,128)S(1)} %copy.68, f32[17,256]{0,1:T(8,128)S(1)} %copy-done.6, pred[17,256]{0,1:T(8,128)(4,1)S(1)} %copy.67), kind=kLoop, calls=%fused_computation.46 | loop fusion | flops 557056 | bytes 1727744 | tf_op jit(solution)/shard_map/sub | solution.py:58
  73.2 2.8 %fusion.1 = f32[16,16,257]{1,0,2:T(8,128)S(1)} fusion(f32[16,16,259]{1,0,2:T(8,128)S(1)} %slice_subtract_fusion, f32[16,16,258]{1,0,2:T(8,128)S(1)} %minimum_add_fusion, f32[16,16,2]{1,0,2:T(8,128)S(1)} %reshape.97, f32[16,16,256]{1,0,2:T(8,128)S(1)} %fusion.14, f32[16,16,2]{1,0,2:T(8,128)S(1)} %reshape.96, f32[16,257]{0,1:T(8,128)S(1)} %copy-done.4, ...), kind=kLoop, calls=%fused_computation.20 | loop fusion | flops 723712 | bytes 1372625 | tf_op jit(solution)/shard_map/jit(_where)/select_n | solution.py:63
  78.2 3.8 %all-to-all-start.1 = ((f32[16,16,1,256]{3,0,2,1:T(8,128)}), f32[16,16,1,256]{3,0,2,1:T(8,128)S(1)}, u32[]{:S(2)}, u32[]{:S(2)}) async-start(f32[16,16,1,256]{3,0,2,1:T(8,128)} %copy.74), calls=%async_computation.1 | async-start | bytes 524288 | tf_op jit(solution)/shard_map/all_to_all | solution.py:121
  82.1 9.7 %all-to-all-done.1 = f32[16,16,1,256]{3,0,2,1:T(8,128)S(1)} async-done(((f32[16,16,1,256]{3,0,2,1:T(8,128)}), f32[16,16,1,256]{3,0,2,1:T(8,128)S(1)}, u32[]{:S(2)}, u32[]{:S(2)}) %all-to-all-start.1) | async-done | bytes 262176 | tf_op jit(solution)/shard_map/all_to_all | solution.py:121
  93.9 2.1 %gather_fusion.1 = f32[768,256]{1,0:T(8,128)S(1)} fusion(f32[256,256]{1,0:T(8,128)S(1)} %bitcast.36, s32[1024]{0:T(1024)S(1)} %pad_clamp_fusion), kind=kCustom, calls=%fused_computation.1.clone | custom fusion | bytes 1575936 | tf_op jit(solution)/shard_map/jit(_take)/gather | solution.py:82
  97.4 2.1 %gather_fusion.2 = f32[768,256]{1,0:T(8,128)S(1)} fusion(f32[256,256]{1,0:T(8,128)S(1)} %fusion.32, s32[1024]{0:T(1024)S(1)} %pad_clamp_fusion.1), kind=kCustom, calls=%fused_computation.2.clone | custom fusion | bytes 1575936 | tf_op jit(solution)/shard_map/jit(_take)/gather | solution.py:81
  99.5 2.1 %gather_fusion.3 = f32[768,256]{1,0:T(8,128)S(1)} fusion(f32[256,256]{1,0:T(8,128)S(1)} %fusion.32, s32[1024]{0:T(1024)S(1)} %pad_clamp_fusion), kind=kCustom, calls=%fused_computation.3.clone | custom fusion | bytes 1575936 | tf_op jit(solution)/shard_map/jit(_take)/gather | solution.py:82
  103.0 2.1 %gather_fusion.4 = f32[768,256]{1,0:T(8,128)S(1)} fusion(f32[256,256]{1,0:T(8,128)S(1)} %fusion.31, s32[1024]{0:T(1024)S(1)} %pad_clamp_fusion.1), kind=kCustom, calls=%fused_computation.4.clone | custom fusion | bytes 1575936 | tf_op jit(solution)/shard_map/jit(_take)/gather | solution.py:81
  105.1 2.1 %gather_fusion.5 = f32[768,256]{1,0:T(8,128)S(1)} fusion(f32[256,256]{1,0:T(8,128)S(1)} %fusion.31, s32[1024]{0:T(1024)S(1)} %pad_clamp_fusion), kind=kCustom, calls=%fused_computation.5.clone | custom fusion | bytes 1575936 | tf_op jit(solution)/shard_map/jit(_take)/gather | solution.py:82
  108.6 2.1 %gather_fusion.6 = f32[768,256]{1,0:T(8,128)S(1)} fusion(f32[256,256]{1,0:T(8,128)S(1)} %fusion.30, s32[1024]{0:T(1024)S(1)} %pad_clamp_fusion.1), kind=kCustom, calls=%fused_computation.6.clone | custom fusion | bytes 1575936 | tf_op jit(solution)/shard_map/jit(_take)/gather | solution.py:81
  110.7 2.1 %gather_fusion.7 = f32[768,256]{1,0:T(8,128)S(1)} fusion(f32[256,256]{1,0:T(8,128)S(1)} %fusion.30, s32[1024]{0:T(1024)S(1)} %pad_clamp_fusion), kind=kCustom, calls=%fused_computation.7.clone | custom fusion | bytes 1575936 | tf_op jit(solution)/shard_map/jit(_take)/gather | solution.py:82
  114.2 2.1 %gather_fusion.8 = f32[768,256]{1,0:T(8,128)S(1)} fusion(f32[256,256]{1,0:T(8,128)S(1)} %fusion.29, s32[1024]{0:T(1024)S(1)} %pad_clamp_fusion.1), kind=kCustom, calls=%fused_computation.8.clone | custom fusion | bytes 1575936 | tf_op jit(solution)/shard_map/jit(_take)/gather | solution.py:81
  116.3 2.4 %gather_fusion.9 = f32[768,256]{1,0:T(8,128)S(1)} fusion(f32[256,256]{1,0:T(8,128)S(1)} %fusion.29, s32[1024]{0:T(1024)S(1)} %pad_clamp_fusion), kind=kCustom, calls=%fused_computation.9.clone | custom fusion | bytes 1575936 | tf_op jit(solution)/shard_map/jit(_take)/gather | solution.py:82
  122.2 2.1 %gather_fusion.11 = f32[768,256]{1,0:T(8,128)S(1)} fusion(f32[256,256]{1,0:T(8,128)S(1)} %fusion.28, s32[1024]{0:T(1024)S(1)} %pad_clamp_fusion), kind=kCustom, calls=%fused_computation.11.clone | custom fusion | bytes 1575936 | tf_op jit(solution)/shard_map/jit(_take)/gather | solution.py:82
  (129 shorter events, 46.2 us)
Async XLA Ops:
  1.3 14.1 %all-to-all-start = ((bf16[16,4,1,256]{3,1,2,0:T(4,128)(2,1)}), bf16[16,4,1,256]{3,1,2,0:T(4,128)(2,1)S(1)}, u32[]{:S(2)}, u32[]{:S(2)}) async-start(bf16[16,4,1,256]{3,1,2,0:T(4,128)(2,1)} %stack.3), calls=%async_computation | async-start | bytes 65536 | tf_op jit(solution)/shard_map/all_to_all | solution.py:97
  15.4 5.3 %collective-permute-start = (f32[20,4,256]{2,1,0:T(4,128)S(1)}, f32[20,4,256]{2,1,0:T(4,128)S(1)}, u32[]{:S(2)}, u32[]{:S(2)}) collective-permute-start(f32[20,4,256]{2,1,0:T(4,128)S(1)} %get-tuple-element.30), channel_id=1, source_target_pairs={{0,1},{1,0},{2,3},{3,2},{4,5},{5,4},{6,7},{7,6},{8,9},{9,8},{10,11... | collective-permute-start | bytes 245768 | tf_op jit(solution)/shard_map/ppermute | solution.py:20
  17.0 4.6 %collective-permute-start.1 = (f32[20,4,256]{2,1,0:T(4,128)S(1)}, f32[20,4,256]{2,1,0:T(4,128)S(1)}, u32[]{:S(2)}, u32[]{:S(2)}) collective-permute-start(f32[20,4,256]{2,1,0:T(4,128)S(1)} %get-tuple-element.31), channel_id=1, source_target_pairs={{1,0},{0,1},{3,2},{2,3},{5,4},{4,5},{7,6},{6,7},{9,8},{8,9},{11,10... | collective-permute-start | bytes 245768 | tf_op jit(solution)/shard_map/ppermute | solution.py:22
  40.3 2.5 %copy-start.13 = (f32[21,256]{1,0:T(8,128)S(1)}, f32[21,256]{1,0:T(8,128)}, u32[]{:S(2)}) copy-start(f32[21,256]{1,0:T(8,128)} %get-tuple-element.44) | copy-start | bytes 64516
  40.4 6.8 %copy-start.7 = (f32[21,256]{0,1:T(8,128)S(1)}, f32[21,256]{0,1:T(8,128)}, u32[]{:S(2)}) copy-start(f32[21,256]{0,1:T(8,128)} %copy.54) | copy-start | bytes 64516
  47.2 4.8 %copy-start.3 = (f32[16,20,256]{1,0,2:T(8,128)S(1)}, f32[16,20,256]{1,0,2:T(8,128)}, u32[]{:S(2)}) copy-start(f32[16,20,256]{1,0,2:T(8,128)} %copy.77) | copy-start | bytes 983044
  52.6 1.3 %copy-start = (f32[16,20,256]{1,0,2:T(8,128)}, f32[16,20,256]{1,0,2:T(8,128)S(1)}, u32[]{:S(2)}) copy-start(f32[16,20,256]{1,0,2:T(8,128)S(1)} %fusion.21) | copy-start | bytes 983044
  54.0 1.7 %copy-start.9 = (f32[20,257]{1,0:T(8,128)S(1)}, f32[20,257]{1,0:T(8,128)}, u32[]{:S(2)}) copy-start(f32[20,257]{1,0:T(8,128)} %get-tuple-element.32) | copy-start | bytes 61684
  54.0 1.8 %copy-start.8 = (f32[20,257]{1,0:T(8,128)S(1)}, f32[20,257]{1,0:T(8,128)}, u32[]{:S(2)}) copy-start(f32[20,257]{1,0:T(8,128)} %get-tuple-element.33) | copy-start | bytes 61684
  54.0 1.9 %copy-start.14 = (pred[20,257]{1,0:T(8,128)(4,1)S(1)}, pred[20,257]{1,0:T(8,128)(4,1)}, u32[]{:S(2)}) copy-start(pred[20,257]{1,0:T(8,128)(4,1)} %get-tuple-element.18) | copy-start | bytes 15424
  54.0 2.1 %copy-start.5 = (f32[20,257]{0,1:T(8,128)S(1)}, f32[20,257]{0,1:T(8,128)}, u32[]{:S(2)}) copy-start(f32[20,257]{0,1:T(8,128)} %copy.62) | copy-start | bytes 61684
  54.0 2.1 %copy-start.19 = (pred[257]{0:T(512)(128)(4,1)S(1)}, pred[257]{0:T(512)(128)(4,1)}, u32[]{:S(2)}) copy-start(pred[257]{0:T(512)(128)(4,1)} %fusion.90) | copy-start | bytes 775
  56.1 6.4 %copy-start.1 = (f32[16,20,256]{1,0,2:T(8,128)S(1)}, f32[16,20,256]{1,0,2:T(8,128)}, u32[]{:S(2)}) copy-start(f32[16,20,256]{1,0,2:T(8,128)} %copy-done) | copy-start | bytes 983044
  63.4 2.0 %copy-start.2 = (f32[16,19,256]{1,0,2:T(8,128)}, f32[16,19,256]{1,0,2:T(8,128)S(1)}, u32[]{:S(2)}) copy-start(f32[16,19,256]{1,0,2:T(8,128)S(1)} %slice_subtract_fusion.4) | copy-start | bytes 933892
  63.4 2.0 %copy-start.12 = (f32[17,256]{1,0:T(8,128)S(1)}, f32[17,256]{1,0:T(8,128)}, u32[]{:S(2)}) copy-start(f32[17,256]{1,0:T(8,128)} %get-tuple-element.42) | copy-start | bytes 52228
  63.4 2.1 %copy-start.11 = (f32[17,256]{1,0:T(8,128)S(1)}, f32[17,256]{1,0:T(8,128)}, u32[]{:S(2)}) copy-start(f32[17,256]{1,0:T(8,128)} %get-tuple-element.43) | copy-start | bytes 52228
  63.4 2.2 %copy-start.15 = (pred[17,256]{1,0:T(8,128)(4,1)S(1)}, pred[17,256]{1,0:T(8,128)(4,1)}, u32[]{:S(2)}) copy-start(pred[17,256]{1,0:T(8,128)(4,1)} %get-tuple-element.16) | copy-start | bytes 13060
  63.4 2.3 %copy-start.6 = (f32[17,256]{0,1:T(8,128)S(1)}, f32[17,256]{0,1:T(8,128)}, u32[]{:S(2)}) copy-start(f32[17,256]{0,1:T(8,128)} %copy.66) | copy-start | bytes 52228
  72.3 0.9 copy-start.4
  76.4 5.6 %copy-start.17 = (s32[768]{0:T(1024)S(1)}, s32[768]{0:T(1024)}, u32[]{:S(2)}) copy-start(s32[768]{0:T(1024)} %get-tuple-element.47) | copy-start | bytes 9220
  76.4 5.6 %copy-start.16 = (s32[768]{0:T(1024)S(1)}, s32[768]{0:T(1024)}, u32[]{:S(2)}) copy-start(s32[768]{0:T(1024)} %get-tuple-element.46) | copy-start | bytes 9220
  76.4 5.6 %copy-start.18 = (s32[768,2]{0,1:T(2,128)S(1)}, s32[768,2]{0,1:T(2,128)}, u32[]{:S(2)}) copy-start(s32[768,2]{0,1:T(2,128)} %param.11) | copy-start | bytes 18436
  78.2 13.5 %all-to-all-start.1 = ((f32[16,16,1,256]{3,0,2,1:T(8,128)}), f32[16,16,1,256]{3,0,2,1:T(8,128)S(1)}, u32[]{:S(2)}, u32[]{:S(2)}) async-start(f32[16,16,1,256]{3,0,2,1:T(8,128)} %copy.74), calls=%async_computation.1 | async-start | bytes 524288 | tf_op jit(solution)/shard_map/all_to_all | solution.py:121
  93.9 2.1 %copy-start.20 = (f32[768]{0:T(1024)S(1)}, f32[768]{0:T(1024)}, u32[]{:S(2)}) copy-start(f32[768]{0:T(1024)} %param.9) | copy-start | bytes 9220
  (1 other events, 0.9 us)
